TPU v7x, 32 devices: a whole 2x2x4 slice. The times are simulated.
32 devices in a mesh: dp: 16 (over z, y, core), seq: 2 (over x).
Axes of the slice: x: 2, y: 2, z: 4, core: 2. Of those that a mesh axis runs over, the one named last changes fastest.
Arguments:
- tokens: bfloat16 [16, 512, 1024], P('dp', 'seq'), may hold values from -6 to 6
- first_values: bfloat16 [16, 512, 1024], P('dp', 'seq'), may hold values from -6 to 6
- doc_ids: int32 [16, 512], P('dp'), may hold values from 0 to 7, never falling along the last dimension, each value on 1 to 256 neighbouring positions
- cotangent: bfloat16 [16, 512, 1024], P('dp', 'seq'), may hold values from -6 to 6
- norm1_gain: bfloat16 [1024], P(('dp', 'seq')), may hold values from 0.5 to 1.5
- w_query: bfloat16 [1024, 1024], P(('dp', 'seq')), may hold values from -0.25 to 0.25
- w_key: bfloat16 [1024, 1024], P(('dp', 'seq')), may hold values from -0.25 to 0.25
- w_value: bfloat16 [1024, 1024], P(('dp', 'seq')), may hold values from -0.1875 to 0.1875
- w_out: bfloat16 [1024, 1024], P(('dp', 'seq')), may hold values from -0.75 to 0.75
- norm2_gain: bfloat16 [1024], P(('dp', 'seq')), may hold values from 0.5 to 1.5
- w_gate: bfloat16 [1024, 2816], P(('dp', 'seq')), may hold values from -0.1875 to 0.1875
- w_up: bfloat16 [1024, 2816], P(('dp', 'seq')), may hold values from -0.1875 to 0.1875
- w_down: bfloat16 [2816, 1024], P(('dp', 'seq')), may hold values from -0.21875 to 0.21875
Outputs:
- layer_out: bfloat16 [16, 512, 1024], P('dp', 'seq')
- grad_tokens: bfloat16 [16, 512, 1024], P('dp', 'seq')
- grad_first_values: bfloat16 [16, 512, 1024], P('dp', 'seq')
- grad_norm1: float32 [1024], P(('dp', 'seq'))
- grad_query: float32 [1024, 1024], P(('dp', 'seq'))
- grad_key: float32 [1024, 1024], P(('dp', 'seq'))
- grad_value: float32 [1024, 1024], P(('dp', 'seq'))
- grad_out: float32 [1024, 1024], P(('dp', 'seq'))
- grad_norm2: float32 [1024], P(('dp', 'seq'))
- grad_gate: float32 [1024, 2816], P(('dp', 'seq'))
- grad_up: float32 [1024, 2816], P(('dp', 'seq'))
- grad_down: float32 [2816, 1024], P(('dp', 'seq'))
Inputs may be any that keep to these rules, and one draw needn't show every extreme that they name: `doc_ids`: along a stream the document numbers never fall; each document covers 1 to 256 positions, and in each stream one covers exactly 256.
All inputs are finite; a program needn't handle non-finite values.
Results may differ from a plain program's by a relative error of at most 0.025.
Values may be sent and summed in bfloat16 or wider, within the bound.
A program may use at most 192 MiB of HBM per device.

v0:
```python
import jax
import jax.numpy as jnp
from jax import lax
from jax.sharding import PartitionSpec as P

H = 16
BLOCK = 512


epsilon = 1e-05


def norm_forward(h, gain):
    inverse = lax.rsqrt(jnp.mean(h * h, axis=-1, keepdims=True) + epsilon)
    return (h * inverse * gain, inverse)


def norm_backward(h, inverse, gain, grad_normed):
    scaled = grad_normed * gain
    grad_gain = jnp.sum(grad_normed * h * inverse, axis=0)
    grad_h = inverse * scaled - h * inverse * inverse * inverse * jnp.mean(
        h * scaled, axis=-1, keepdims=True
    )
    return (grad_h, grad_gain)


def rope_tables(start, count, width):
    positions = (start + jnp.arange(count, dtype=jnp.int32)).astype(jnp.float32)
    freqs = 10000.0 ** (-jnp.arange(width // 2, dtype=jnp.float32) * 2.0 / width)
    angle = positions[:, None] * freqs[None, :]
    return (jnp.cos(angle)[:, None, :], jnp.sin(angle)[:, None, :])


def rotate(t, cos_tab, sin_tab, sign):
    half = t.shape[-1] // 2
    first = t[..., :half]
    second = t[..., half:]
    return jnp.concatenate(
        [first * cos_tab - sign * second * sin_tab, sign * first * sin_tab + second * cos_tab],
        axis=-1,
    )


def seq_major(t, outer, inner):
    shape = t.shape
    lead = (outer, inner, shape[0] // (outer * inner)) + tuple(shape[1:])
    return jnp.swapaxes(t.reshape(lead), 0, 1).reshape(shape)


def matmul_left(a, b):
    return lax.dot_general(a, b, (((0,), (0,)), ((), ())), preferred_element_type=jnp.float32)


def matmul_right(a, b):
    return lax.dot_general(a, b, (((1,), (1,)), ((), ())), preferred_element_type=jnp.float32)


def per_device(
    tokens,
    first_values,
    doc_ids,
    cotangent,
    norm1_gain,
    w_query,
    w_key,
    w_value,
    w_out,
    norm2_gain,
    w_gate,
    w_up,
    w_down,
):
    groups = lax.axis_size("seq")
    outer = lax.axis_size("dp")
    rows = tokens.shape[1]
    width = tokens.shape[2]
    head_size = width // H
    local_heads = H // groups
    stream_len = rows * groups
    scale = head_size ** (-0.5)
    block_count = stream_len // BLOCK
    x_in = tokens[0].astype(jnp.float32)
    segment = doc_ids[0]
    attn_set = (
        lax.all_gather(norm1_gain, ("dp", "seq"), axis=0, tiled=True),
        lax.all_gather(w_query, ("dp", "seq"), axis=0, tiled=True),
        lax.all_gather(w_key, ("dp", "seq"), axis=0, tiled=True),
        lax.all_gather(w_value, ("dp", "seq"), axis=0, tiled=True),
        lax.all_gather(w_out, ("dp", "seq"), axis=0, tiled=True),
    )
    gain1, wq, wk, wv, wo = attn_set
    gain1_f = gain1.astype(jnp.float32)
    normed1, inverse1 = norm_forward(x_in, gain1_f)
    normed1_b = normed1.astype(jnp.bfloat16)
    cos_tab, sin_tab = rope_tables(lax.axis_index("seq") * rows, rows, head_size)

    def project(weight):
        return jnp.dot(normed1_b, weight, preferred_element_type=jnp.float32).reshape(
            rows, H, head_size
        )

    query_b = rotate(project(wq), cos_tab, sin_tab, 1.0).astype(jnp.bfloat16)
    key_b = rotate(project(wk), cos_tab, sin_tab, 1.0).astype(jnp.bfloat16)
    first_f = first_values[0].astype(jnp.float32).reshape(rows, H, head_size)
    value_b = (0.5 * (project(wv) + first_f)).astype(jnp.bfloat16)

    def slice_layout(t):
        return t.reshape(rows, groups, local_heads * head_size)

    def head_layout(t):
        return t.reshape(stream_len, local_heads, head_size)

    query_h, key_h, value_h = (
        lax.all_to_all(slice_layout(query_b), "seq", split_axis=1, concat_axis=0, tiled=True),
        lax.all_to_all(slice_layout(key_b), "seq", split_axis=1, concat_axis=0, tiled=True),
        lax.all_to_all(slice_layout(value_b), "seq", split_axis=1, concat_axis=0, tiled=True),
    )
    query_h = head_layout(query_h)
    key_h = head_layout(key_h)
    value_h = head_layout(value_h)
    positions = jnp.arange(stream_len, dtype=jnp.int32)

    def block_scores(q_rows, start):
        seg_rows = lax.dynamic_slice_in_dim(segment, start, BLOCK, 0)
        pos_rows = start + jnp.arange(BLOCK, dtype=jnp.int32)
        mask = (seg_rows[:, None] == segment[None, :]) & (positions[None, :] <= pos_rows[:, None])
        raw = jnp.einsum("qhd,khd->hqk", q_rows, key_h, preferred_element_type=jnp.float32) * scale
        return jnp.where(mask[None], raw, -1e30)

    def attend(start):
        q_rows = lax.dynamic_slice_in_dim(query_h, start, BLOCK, 0)
        scores = block_scores(q_rows, start)
        peak = jnp.max(scores, axis=-1, keepdims=True)
        expo = jnp.exp(scores - peak)
        total = jnp.sum(expo, axis=-1, keepdims=True)
        probs_b = (expo / total).astype(jnp.bfloat16)
        mixed_rows = jnp.einsum(
            "hqk,khd->qhd", probs_b, value_h, preferred_element_type=jnp.float32
        ).astype(jnp.bfloat16)
        return (mixed_rows, (peak + jnp.log(total))[..., 0])

    starts = jnp.arange(block_count, dtype=jnp.int32) * BLOCK
    mixed_h, log_totals = lax.map(attend, starts)
    mixed_h = mixed_h.reshape(stream_len, 1, local_heads * head_size)
    mixed_b = lax.all_to_all(mixed_h, "seq", split_axis=0, concat_axis=1, tiled=True).reshape(
        rows, width
    )
    h1 = x_in + jnp.dot(mixed_b, wo, preferred_element_type=jnp.float32)
    ffn_set = (
        lax.all_gather(norm2_gain, ("dp", "seq"), axis=0, tiled=True),
        lax.all_gather(w_gate, ("dp", "seq"), axis=0, tiled=True),
        lax.all_gather(w_up, ("dp", "seq"), axis=0, tiled=True),
        lax.all_gather(w_down, ("dp", "seq"), axis=0, tiled=True),
    )
    gain2, wg, wu, wd = ffn_set
    gain2_f = gain2.astype(jnp.float32)
    normed2, inverse2 = norm_forward(h1, gain2_f)
    normed2_b = normed2.astype(jnp.bfloat16)
    gate = jnp.dot(normed2_b, wg, preferred_element_type=jnp.float32)
    up_proj = jnp.dot(normed2_b, wu, preferred_element_type=jnp.float32)
    sigma = jax.nn.sigmoid(gate)
    active = gate * sigma
    hidden_b = (active * up_proj).astype(jnp.bfloat16)
    result = h1 + jnp.dot(hidden_b, wd, preferred_element_type=jnp.float32)
    layer_out = result.astype(jnp.bfloat16).reshape(1, rows, width)
    again_attn = (
        lax.all_gather(norm1_gain, ("dp", "seq"), axis=0, tiled=True),
        lax.all_gather(w_query, ("dp", "seq"), axis=0, tiled=True),
        lax.all_gather(w_key, ("dp", "seq"), axis=0, tiled=True),
        lax.all_gather(w_value, ("dp", "seq"), axis=0, tiled=True),
        lax.all_gather(w_out, ("dp", "seq"), axis=0, tiled=True),
    )
    wq2, wk2, wv2, wo2 = (again_attn[1], again_attn[2], again_attn[3], again_attn[4])
    again_ffn = (
        lax.all_gather(norm2_gain, ("dp", "seq"), axis=0, tiled=True),
        lax.all_gather(w_gate, ("dp", "seq"), axis=0, tiled=True),
        lax.all_gather(w_up, ("dp", "seq"), axis=0, tiled=True),
        lax.all_gather(w_down, ("dp", "seq"), axis=0, tiled=True),
    )
    wg2, wu2, wd2 = (again_ffn[1], again_ffn[2], again_ffn[3])
    grad_y_b = cotangent[0]
    grad_y = grad_y_b.astype(jnp.float32)
    grad_wd = matmul_left(hidden_b, grad_y_b)
    grad_hidden = matmul_right(grad_y_b, wd2)
    grad_gate_b = (grad_hidden * up_proj * sigma * (1.0 + gate * (1.0 - sigma))).astype(
        jnp.bfloat16
    )
    grad_up_b = (grad_hidden * active).astype(jnp.bfloat16)
    grad_wg = matmul_left(normed2_b, grad_gate_b)
    grad_wu = matmul_left(normed2_b, grad_up_b)
    grad_n2 = matmul_right(grad_gate_b, wg2) + matmul_right(grad_up_b, wu2)
    grad_h1_norm, grad_g2 = norm_backward(h1, inverse2, gain2_f, grad_n2)
    grad_h1 = grad_y + grad_h1_norm
    grad_att_b = grad_h1.astype(jnp.bfloat16)
    grad_wo = matmul_left(mixed_b, grad_att_b)
    grad_mixed_b = matmul_right(grad_att_b, wo2).astype(jnp.bfloat16)
    grad_mixed_h = head_layout(
        lax.all_to_all(slice_layout(grad_mixed_b), "seq", split_axis=1, concat_axis=0, tiled=True)
    )

    def attend_back(carry, item):
        acc_key, acc_value = carry
        start, lse_rows = item
        q_rows = lax.dynamic_slice_in_dim(query_h, start, BLOCK, 0)
        d_rows = lax.dynamic_slice_in_dim(grad_mixed_h, start, BLOCK, 0)
        probs = jnp.exp(block_scores(q_rows, start) - lse_rows[..., None])
        grad_probs = jnp.einsum("qhd,khd->hqk", d_rows, value_h, preferred_element_type=jnp.float32)
        inner = jnp.sum(probs * grad_probs, axis=-1, keepdims=True)
        grad_scores = (probs * (grad_probs - inner)).astype(jnp.bfloat16)
        grad_q_rows = (
            jnp.einsum("hqk,khd->qhd", grad_scores, key_h, preferred_element_type=jnp.float32)
            * scale
        ).astype(jnp.bfloat16)
        acc_key = (
            acc_key
            + jnp.einsum("hqk,qhd->khd", grad_scores, q_rows, preferred_element_type=jnp.float32)
            * scale
        )
        acc_value = acc_value + jnp.einsum(
            "hqk,qhd->khd", probs.astype(jnp.bfloat16), d_rows, preferred_element_type=jnp.float32
        )
        return ((acc_key, acc_value), grad_q_rows)

    empty = jnp.zeros((stream_len, local_heads, head_size), jnp.float32)
    (acc_key, acc_value), grad_q_h = lax.scan(attend_back, (empty, empty), (starts, log_totals))
    flat_width = local_heads * head_size
    grad_q_h = grad_q_h.reshape(stream_len, 1, flat_width)
    grad_k_h = acc_key.astype(jnp.bfloat16).reshape(stream_len, 1, flat_width)
    grad_v_h = acc_value.astype(jnp.bfloat16).reshape(stream_len, 1, flat_width)
    grad_q_s, grad_k_s, grad_v_s = (
        lax.all_to_all(grad_q_h, "seq", split_axis=0, concat_axis=1, tiled=True),
        lax.all_to_all(grad_k_h, "seq", split_axis=0, concat_axis=1, tiled=True),
        lax.all_to_all(grad_v_h, "seq", split_axis=0, concat_axis=1, tiled=True),
    )

    def unrotate(t):
        heads_form = t.astype(jnp.float32).reshape(rows, H, head_size)
        return rotate(heads_form, cos_tab, sin_tab, -1.0).astype(jnp.bfloat16).reshape(rows, width)

    grad_qlin_b = unrotate(grad_q_s)
    grad_klin_b = unrotate(grad_k_s)
    half_value = (0.5 * grad_v_s.astype(jnp.float32).reshape(rows, width)).astype(jnp.bfloat16)
    grad_first = half_value.reshape(1, rows, width)
    grad_wq = matmul_left(normed1_b, grad_qlin_b)
    grad_wk = matmul_left(normed1_b, grad_klin_b)
    grad_wv = matmul_left(normed1_b, half_value)
    grad_n1 = (
        matmul_right(grad_qlin_b, wq2)
        + matmul_right(grad_klin_b, wk2)
        + matmul_right(half_value, wv2)
    )
    grad_x_norm, grad_g1 = norm_backward(x_in, inverse1, gain1_f, grad_n1)
    grad_tokens = (grad_h1 + grad_x_norm).astype(jnp.bfloat16).reshape(1, rows, width)
    attn_part = (
        lax.psum_scatter(
            seq_major(grad_g1, outer, groups).astype(jnp.bfloat16),
            "seq",
            scatter_dimension=0,
            tiled=True,
        ).astype(jnp.float32),
        lax.psum_scatter(
            seq_major(grad_wq, outer, groups).astype(jnp.bfloat16),
            "seq",
            scatter_dimension=0,
            tiled=True,
        ).astype(jnp.float32),
        lax.psum_scatter(
            seq_major(grad_wk, outer, groups).astype(jnp.bfloat16),
            "seq",
            scatter_dimension=0,
            tiled=True,
        ).astype(jnp.float32),
        lax.psum_scatter(
            seq_major(grad_wv, outer, groups).astype(jnp.bfloat16),
            "seq",
            scatter_dimension=0,
            tiled=True,
        ).astype(jnp.float32),
        lax.psum_scatter(
            seq_major(grad_wo, outer, groups).astype(jnp.bfloat16),
            "seq",
            scatter_dimension=0,
            tiled=True,
        ).astype(jnp.float32),
    )
    attn_red = (
        lax.psum_scatter(
            attn_part[0].astype(jnp.bfloat16), "dp", scatter_dimension=0, tiled=True
        ).astype(jnp.float32),
        lax.psum_scatter(
            attn_part[1].astype(jnp.bfloat16), "dp", scatter_dimension=0, tiled=True
        ).astype(jnp.float32),
        lax.psum_scatter(
            attn_part[2].astype(jnp.bfloat16), "dp", scatter_dimension=0, tiled=True
        ).astype(jnp.float32),
        lax.psum_scatter(
            attn_part[3].astype(jnp.bfloat16), "dp", scatter_dimension=0, tiled=True
        ).astype(jnp.float32),
        lax.psum_scatter(
            attn_part[4].astype(jnp.bfloat16), "dp", scatter_dimension=0, tiled=True
        ).astype(jnp.float32),
    )
    ffn_part = (
        lax.psum_scatter(
            seq_major(grad_g2, outer, groups).astype(jnp.bfloat16),
            "seq",
            scatter_dimension=0,
            tiled=True,
        ).astype(jnp.float32),
        lax.psum_scatter(
            seq_major(grad_wg, outer, groups).astype(jnp.bfloat16),
            "seq",
            scatter_dimension=0,
            tiled=True,
        ).astype(jnp.float32),
        lax.psum_scatter(
            seq_major(grad_wu, outer, groups).astype(jnp.bfloat16),
            "seq",
            scatter_dimension=0,
            tiled=True,
        ).astype(jnp.float32),
        lax.psum_scatter(
            seq_major(grad_wd, outer, groups).astype(jnp.bfloat16),
            "seq",
            scatter_dimension=0,
            tiled=True,
        ).astype(jnp.float32),
    )
    ffn_red = (
        lax.psum_scatter(
            ffn_part[0].astype(jnp.bfloat16), "dp", scatter_dimension=0, tiled=True
        ).astype(jnp.float32),
        lax.psum_scatter(
            ffn_part[1].astype(jnp.bfloat16), "dp", scatter_dimension=0, tiled=True
        ).astype(jnp.float32),
        lax.psum_scatter(
            ffn_part[2].astype(jnp.bfloat16), "dp", scatter_dimension=0, tiled=True
        ).astype(jnp.float32),
        lax.psum_scatter(
            ffn_part[3].astype(jnp.bfloat16), "dp", scatter_dimension=0, tiled=True
        ).astype(jnp.float32),
    )
    return (
        layer_out,
        grad_tokens,
        grad_first,
        attn_red[0],
        attn_red[1],
        attn_red[2],
        attn_red[3],
        attn_red[4],
        ffn_red[0],
        ffn_red[1],
        ffn_red[2],
        ffn_red[3],
    )


def solution(mesh):
    placed = (
        P("dp", "seq", None),
        P("dp", "seq", None),
        P("dp", None),
        P("dp", "seq", None),
        P(("dp", "seq")),
        P(("dp", "seq"), None),
        P(("dp", "seq"), None),
        P(("dp", "seq"), None),
        P(("dp", "seq"), None),
        P(("dp", "seq")),
        P(("dp", "seq"), None),
        P(("dp", "seq"), None),
        P(("dp", "seq"), None),
    )
    return jax.shard_map(
        per_device,
        mesh=mesh,
        in_specs=placed,
        out_specs=(
            P("dp", "seq", None),
            P("dp", "seq", None),
            P("dp", "seq", None),
            P(("dp", "seq")),
            P(("dp", "seq"), None),
            P(("dp", "seq"), None),
            P(("dp", "seq"), None),
            P(("dp", "seq"), None),
            P(("dp", "seq")),
            P(("dp", "seq"), None),
            P(("dp", "seq"), None),
            P(("dp", "seq"), None),
        ),
        check_vma=False,
    )
```

profile of v0, /device:TPU:0, one launch (start us, length us, event | category | flops | bytes accessed | tf_op | source)
XLA Modules:
  0.0 1361.9 jit_solution(14809895910916897110)
XLA Ops:
  13.6 42.2 %all-reduce.6 = (bf16[1024]{0:T(1024)(128)(2,1)S(1)}, bf16[1024]{0:T(1024)(128)(2,1)S(1)}) all-reduce(bf16[1024]{0:T(1024)(128)(2,1)S(1)} %dynamic-update-slice, bf16[1024]{0:T(1024)(128)(2,1)S(1)} %dynamic-update-slice.1), channel_id=1, replica_groups=mesh['dp'=16,'seq'=2] {'dp','seq'}, use_global_device_ids=true, to_apply=%add | all-reduce | flops 2048 | bytes 8192
  58.5 11.7 all-gather.8.cloned.1.call-done
  70.2 4.0 copy.179
  74.2 3.2 fusion.19
  77.4 3.5 all-to-all-start
  80.9 47.7 %all-gather.12.cloned.1.call-done = bf16[1024,1024]{1,0:T(8,128)(2,1)} async-done(((bf16[32,1024]{1,0:T(8,128)(2,1)}), bf16[1024,1024]{1,0:T(8,128)(2,1)}) %all-gather.12.cloned.1.call-update) | async-done | bytes 2097168 | tf_op jit(solution)/shard_map/all_gather | solution.py:87
  128.5 4.0 copy.184
  132.5 54.3 %all-gather.10.cloned.1.call-done = bf16[1024,1024]{1,0:T(8,128)(2,1)} async-done(((bf16[32,1024]{1,0:T(8,128)(2,1)}), bf16[1024,1024]{1,0:T(8,128)(2,1)}) %all-gather.10.cloned.1.call-update) | async-done | bytes 2097168 | tf_op jit(solution)/shard_map/all_gather | solution.py:86
  186.8 3.9 copy.182
  195.3 3.5 all-to-all-start.2
  199.6 7.8 all-to-all-done.2
  207.4 3.8 all-to-all-start.1
  213.2 7.6 all-to-all-done.1
  230.9 4.0 all-to-all-start.3
  235.0 7.2 all-to-all-done.3
  243.0 3.8 all-gather.14.cloned.1.call-done
  249.4 66.5 %all-gather.16.cloned.1.call-done = bf16[1024,2816]{1,0:T(8,128)(2,1)} async-done(((bf16[32,2816]{1,0:T(8,128)(2,1)}), bf16[1024,2816]{1,0:T(8,128)(2,1)}) %all-gather.16.cloned.1.call-update) | async-done | bytes 5767184 | tf_op jit(solution)/shard_map/all_gather | solution.py:151
  315.9 5.9 fusion.60
  321.8 62.8 %all-gather.18.cloned.1.call-done = bf16[1024,2816]{1,0:T(8,128)(2,1)} async-done(((bf16[32,2816]{1,0:T(8,128)(2,1)}), bf16[1024,2816]{1,0:T(8,128)(2,1)}) %all-gather.18.cloned.1.call-update) | async-done | bytes 5767184 | tf_op jit(solution)/shard_map/all_gather | solution.py:152
  384.6 7.2 fusion.6
  391.8 61.7 %all-gather.20.cloned.1.call-done = bf16[2816,1024]{1,0:T(8,128)(2,1)} async-done(((bf16[88,1024]{1,0:T(8,128)(2,1)}), bf16[2816,1024]{1,0:T(8,128)(2,1)}) %all-gather.20.cloned.1.call-update) | async-done | bytes 5767184 | tf_op jit(solution)/shard_map/all_gather | solution.py:153
  453.5 6.9 multiply_convert_fusion.1
  469.2 4.2 all-to-all-start.4
  476.9 5.3 all-to-all-done.4
  486.4 5.8 fusion.21
  492.2 8.4 multiply_reduce_fusion
  507.5 4.2 all-to-all-start.7
  511.8 6.7 multiply_convert_fusion
  529.0 4.2 all-to-all-start.5
  533.2 4.5 fusion.25
  554.4 4.2 all-to-all-start.6
  605.8 3.1 copy.216
  609.6 8.7 reduce-scatter.23.cloned.1.call-done
  618.3 34.0 %reduce-scatter.19.cloned.1.call-done = bf16[512,1024]{1,0:T(8,128)(2,1)} async-done(((bf16[1024,1024]{1,0:T(8,128)(2,1)}), bf16[512,1024]{1,0:T(8,128)(2,1)}) %reduce-scatter.19.cloned.1.call-update) | async-done | bytes 1048592 | tf_op jit(solution)/shard_map/reduce_scatter | solution.py:267
  652.4 34.1 %reduce-scatter.15.cloned.1.call-done = bf16[512,1024]{1,0:T(8,128)(2,1)} async-done(((bf16[1024,1024]{1,0:T(8,128)(2,1)}), bf16[512,1024]{1,0:T(8,128)(2,1)}) %reduce-scatter.15.cloned.1.call-update) | async-done | bytes 1048592 | tf_op jit(solution)/shard_map/reduce_scatter | solution.py:261
  686.5 73.6 %reduce-scatter.35.cloned.1.call-done = bf16[512,2816]{1,0:T(8,128)(2,1)} async-done(((bf16[1024,2816]{1,0:T(8,128)(2,1)}), bf16[512,2816]{1,0:T(8,128)(2,1)}) %reduce-scatter.35.cloned.1.call-update) | async-done | bytes 2883600 | tf_op jit(solution)/shard_map/reduce_scatter | solution.py:316
  760.2 73.7 %reduce-scatter.31.cloned.1.call-done = bf16[512,2816]{1,0:T(8,128)(2,1)} async-done(((bf16[1024,2816]{1,0:T(8,128)(2,1)}), bf16[512,2816]{1,0:T(8,128)(2,1)}) %reduce-scatter.31.cloned.1.call-update) | async-done | bytes 2883600 | tf_op jit(solution)/shard_map/reduce_scatter | solution.py:310
  834.0 73.6 %reduce-scatter.39.cloned.1.call-done = bf16[1408,1024]{1,0:T(8,128)(2,1)} async-done(((bf16[2816,1024]{1,0:T(8,128)(2,1)}), bf16[1408,1024]{1,0:T(8,128)(2,1)}) %reduce-scatter.39.cloned.1.call-update) | async-done | bytes 2883600 | tf_op jit(solution)/shard_map/reduce_scatter | solution.py:322
  910.2 6.9 fusion.28
  918.6 4.9 all-reduce.8
  923.6 32.0 %all-reduce.7 = (bf16[512]{0:T(512)(128)(2,1)S(1)}, bf16[512]{0:T(512)(128)(2,1)S(1)}) all-reduce(bf16[512]{0:T(512)(128)(2,1)S(1)} %dynamic-slice.1, bf16[512]{0:T(512)(128)(2,1)S(1)} %dynamic-slice.5), channel_id=3, replica_groups=mesh['dp'=16,'seq'=2] {'dp'}, use_global_device_ids=true, to_apply=%region_9.10.clone | all-reduce | flops 1024 | bytes 4096
  956.8 12.0 reduce-scatter.29.cloned.1.call-done
  970.2 58.6 %reduce-scatter.25.cloned.1.call-done = bf16[32,1024]{1,0:T(8,128)(2,1)} async-done(((bf16[512,1024]{1,0:T(8,128)(2,1)}), bf16[32,1024]{1,0:T(8,128)(2,1)}) %reduce-scatter.25.cloned.1.call-update) | async-done | bytes 65552 | tf_op jit(solution)/shard_map/reduce_scatter | solution.py:296
  1030.4 58.6 %reduce-scatter.21.cloned.1.call-done = bf16[32,1024]{1,0:T(8,128)(2,1)} async-done(((bf16[512,1024]{1,0:T(8,128)(2,1)}), bf16[32,1024]{1,0:T(8,128)(2,1)}) %reduce-scatter.21.cloned.1.call-update) | async-done | bytes 65552 | tf_op jit(solution)/shard_map/reduce_scatter | solution.py:293
  1090.4 58.6 %reduce-scatter.17.cloned.1.call-done = bf16[32,1024]{1,0:T(8,128)(2,1)} async-done(((bf16[512,1024]{1,0:T(8,128)(2,1)}), bf16[32,1024]{1,0:T(8,128)(2,1)}) %reduce-scatter.17.cloned.1.call-update) | async-done | bytes 65552 | tf_op jit(solution)/shard_map/reduce_scatter | solution.py:290
  1150.6 66.6 %reduce-scatter.37.cloned.1.call-done = bf16[32,2816]{1,0:T(8,128)(2,1)} async-done(((bf16[512,2816]{1,0:T(8,128)(2,1)}), bf16[32,2816]{1,0:T(8,128)(2,1)}) %reduce-scatter.37.cloned.1.call-update) | async-done | bytes 180240 | tf_op jit(solution)/shard_map/reduce_scatter | solution.py:336
  1218.8 66.3 %reduce-scatter.33.cloned.1.call-done = bf16[32,2816]{1,0:T(8,128)(2,1)} async-done(((bf16[512,2816]{1,0:T(8,128)(2,1)}), bf16[32,2816]{1,0:T(8,128)(2,1)}) %reduce-scatter.33.cloned.1.call-update) | async-done | bytes 180240 | tf_op jit(solution)/shard_map/reduce_scatter | solution.py:333
  1286.8 66.3 %reduce-scatter.41.cloned.1.call-done = bf16[88,1024]{1,0:T(8,128)(2,1)} async-done(((bf16[1408,1024]{1,0:T(8,128)(2,1)}), bf16[88,1024]{1,0:T(8,128)(2,1)}) %reduce-scatter.41.cloned.1.call-update) | async-done | bytes 180240 | tf_op jit(solution)/shard_map/reduce_scatter | solution.py:339
  (227 shorter events, 143.1 us)
Async XLA Ops:
  7.2 63.0 %all-gather.8.cloned.1.call-start = ((), (), s32[]{:S(2)}) async-start(), calls=%async_computation.22 | async-start | bytes 2162688 | tf_op jit(solution)/shard_map/all_gather | solution.py:88
  7.9 120.6 %all-gather.12.cloned.1.call-start = ((), (), s32[]{:S(2)}) async-start(), calls=%async_computation.24 | async-start | bytes 2162688 | tf_op jit(solution)/shard_map/all_gather | solution.py:87
  8.7 178.1 %all-gather.10.cloned.1.call-start = ((), (), s32[]{:S(2)}) async-start(), calls=%async_computation.23 | async-start | bytes 2162688 | tf_op jit(solution)/shard_map/all_gather | solution.py:86
  9.4 237.4 %all-gather.14.cloned.1.call-start = ((), (), s32[]{:S(2)}) async-start(), calls=%async_computation.25 | async-start | bytes 2162688 | tf_op jit(solution)/shard_map/all_gather | solution.py:89
  10.0 305.9 %all-gather.16.cloned.1.call-start = ((), (), s32[]{:S(2)}) async-start(), calls=%async_computation.26 | async-start | bytes 5947392 | tf_op jit(solution)/shard_map/all_gather | solution.py:151
  10.6 374.1 %all-gather.18.cloned.1.call-start = ((), (), s32[]{:S(2)}) async-start(), calls=%async_computation.27 | async-start | bytes 5947392 | tf_op jit(solution)/shard_map/all_gather | solution.py:152
  11.1 442.4 %all-gather.20.cloned.1.call-start = ((), (), s32[]{:S(2)}) async-start(), calls=%async_computation.28 | async-start | bytes 5947392 | tf_op jit(solution)/shard_map/all_gather | solution.py:153
  55.7 18.4 %copy-start.5 = (bf16[1,256,1024]{2,1,0:T(8,128)(2,1)S(1)}, bf16[1,256,1024]{2,1,0:T(8,128)(2,1)}, u32[]{:S(2)}) copy-start(bf16[1,256,1024]{2,1,0:T(8,128)(2,1)} %param.13) | copy-start | bytes 1572868
  77.4 117.9 %all-to-all-start = ((bf16[256,2,512]{0,2,1:T(8,128)(2,1)}), bf16[256,2,512]{0,2,1:T(8,128)(2,1)S(1)}, u32[]{:S(2)}, u32[]{:S(2)}) async-start(bf16[256,2,512]{0,2,1:T(8,128)(2,1)} %bitcast.6), calls=%async_computation | async-start | bytes 1048576 | tf_op jit(solution)/shard_map/all_to_all | solution.py:116
  190.7 2.6 copy-start.21
  194.4 16.8 %copy-start.29 = (s32[1,512]{1,0:T(1,128)S(1)}, s32[1,512]{1,0:T(1,128)}, u32[]{:S(2)}) copy-start(s32[1,512]{1,0:T(1,128)} %param.15) | copy-start | bytes 6148
  195.3 12.1 all-to-all-start.2
  207.4 13.4 all-to-all-start.1
  212.3 12.1 copy-start.18
  213.2 10.0 copy-start.8
  223.2 3.3 copy-start
  230.9 11.3 all-to-all-start.3
  243.0 6.4 copy-start.10
  321.8 131.7 %copy-start.22 = (bf16[1,256,1024]{2,1,0:T(8,128)(2,1)S(1)}, bf16[1,256,1024]{2,1,0:T(8,128)(2,1)}, u32[]{:S(2)}) copy-start(bf16[1,256,1024]{2,1,0:T(8,128)(2,1)} %param.16) | copy-start | bytes 1572868
  453.5 6.9 copy-start.30
  460.4 3.7 copy-start.31
  469.2 13.0 all-to-all-start.4
  473.4 135.6 %reduce-scatter.27.cloned.1.call-start = ((), (), s32[]{:S(2)}) async-start(), calls=%async_computation.35 | async-start | bytes 3145728 | tf_op jit(solution)/shard_map/reduce_scatter | solution.py:279
  486.4 5.8 copy-start.11
  486.4 5.8 copy-start.19
  507.5 21.5 %all-to-all-start.7 = ((bf16[2,2,65536]{2,1,0:T(2,128)(2,1)}), bf16[2,2,65536]{2,1,0:T(2,128)(2,1)}, u32[]{:S(2)}, u32[]{:S(2)}) async-start(bf16[2,2,65536]{2,1,0:T(2,128)(2,1)} %reshape.425), calls=%async_computation.7 | async-start | bytes 1048576 | tf_op jit(solution)/shard_map/all_to_all | solution.py:233
  511.7 8.8 copy-start.9
  518.5 2.0 copy-start.1
  529.0 25.4 %all-to-all-start.5 = ((bf16[2,2,65536]{2,1,0:T(2,128)(2,1)}), bf16[2,2,65536]{2,1,0:T(2,128)(2,1)}, u32[]{:S(2)}, u32[]{:S(2)}) async-start(bf16[2,2,65536]{2,1,0:T(2,128)(2,1)} %reshape.421), calls=%async_computation.5 | async-start | bytes 1048576 | tf_op jit(solution)/shard_map/all_to_all | solution.py:231
  554.4 12.1 all-to-all-start.6
  558.6 59.6 %reduce-scatter.23.cloned.1.call-start = ((), (), s32[]{:S(2)}) async-start(), calls=%async_computation.33 | async-start | bytes 3145728 | tf_op jit(solution)/shard_map/reduce_scatter | solution.py:273
  573.9 2.9 copy-start.4
  576.0 2.7 copy-start.16
  586.3 66.0 %reduce-scatter.19.cloned.1.call-start = ((), (), s32[]{:S(2)}) async-start(), calls=%async_computation.31 | async-start | bytes 3145728 | tf_op jit(solution)/shard_map/reduce_scatter | solution.py:267
  588.6 97.9 %reduce-scatter.15.cloned.1.call-start = ((), (), s32[]{:S(2)}) async-start(), calls=%async_computation.29 | async-start | bytes 3145728 | tf_op jit(solution)/shard_map/reduce_scatter | solution.py:261
  591.0 169.2 %reduce-scatter.35.cloned.1.call-start = ((), (), s32[]{:S(2)}) async-start(), calls=%async_computation.39 | async-start | bytes 8650752 | tf_op jit(solution)/shard_map/reduce_scatter | solution.py:316
  596.0 237.9 %reduce-scatter.31.cloned.1.call-start = ((), (), s32[]{:S(2)}) async-start(), calls=%async_computation.37 | async-start | bytes 8650752 | tf_op jit(solution)/shard_map/reduce_scatter | solution.py:310
  602.1 305.4 %reduce-scatter.39.cloned.1.call-start = ((), (), s32[]{:S(2)}) async-start(), calls=%async_computation.41 | async-start | bytes 8650752 | tf_op jit(solution)/shard_map/reduce_scatter | solution.py:322
  608.9 359.8 %reduce-scatter.29.cloned.1.call-start = ((), (), s32[]{:S(2)}) async-start(), calls=%async_computation.36 | async-start | bytes 1114112 | tf_op jit(solution)/shard_map/reduce_scatter | solution.py:299
  609.5 419.3 %reduce-scatter.25.cloned.1.call-start = ((), (), s32[]{:S(2)}) async-start(), calls=%async_computation.34 | async-start | bytes 1114112 | tf_op jit(solution)/shard_map/reduce_scatter | solution.py:296
  618.3 470.6 %reduce-scatter.21.cloned.1.call-start = ((), (), s32[]{:S(2)}) async-start(), calls=%async_computation.32 | async-start | bytes 1114112 | tf_op jit(solution)/shard_map/reduce_scatter | solution.py:293
  652.3 496.7 %reduce-scatter.17.cloned.1.call-start = ((), (), s32[]{:S(2)}) async-start(), calls=%async_computation.30 | async-start | bytes 1114112 | tf_op jit(solution)/shard_map/reduce_scatter | solution.py:290
  686.5 530.6 %reduce-scatter.37.cloned.1.call-start = ((), (), s32[]{:S(2)}) async-start(), calls=%async_computation.40 | async-start | bytes 3063808 | tf_op jit(solution)/shard_map/reduce_scatter | solution.py:336
  760.1 525.0 %reduce-scatter.33.cloned.1.call-start = ((), (), s32[]{:S(2)}) async-start(), calls=%async_computation.38 | async-start | bytes 3063808 | tf_op jit(solution)/shard_map/reduce_scatter | solution.py:333
  833.9 73.7 %copy-start.33 = (u32[32]{0:T(128)S(1)}, u32[32]{0:T(128)}, u32[]{:S(2)}) copy-start(u32[32]{0:T(128)} %constant.97) | copy-start | bytes 388
  833.9 74.9 %copy-start.32 = (u32[32]{0:T(128)S(1)}, u32[32]{0:T(128)}, u32[]{:S(2)}) copy-start(u32[32]{0:T(128)} %constant.93) | copy-start | bytes 388
  833.9 519.2 %reduce-scatter.41.cloned.1.call-start = ((), (), s32[]{:S(2)}) async-start(), calls=%async_computation.42 | async-start | bytes 3063808 | tf_op jit(solution)/shard_map/reduce_scatter | solution.py:339
  910.2 7.0 copy-start.13
  (15 other events, 24.0 us)
Sparse Core Ops, SparseCore 0:
  11.0 59.1 all-gather.7
  73.2 55.3 all-gather.11
  131.5 55.1 all-gather.9
  189.6 57.1 all-gather.13
  249.6 66.2 all-gather.15
  318.6 65.9 all-gather.17
  387.5 65.9 all-gather.19
  477.0 31.9 reduce-scatter.26
  586.4 31.7 reduce-scatter.22
  620.3 31.8 reduce-scatter.18
  654.5 31.8 reduce-scatter.14
  688.6 71.4 reduce-scatter.34
  762.4 71.4 reduce-scatter.30
  836.1 71.4 reduce-scatter.38
  911.0 57.6 reduce-scatter.28
  972.2 56.5 reduce-scatter.24
  1032.3 56.5 reduce-scatter.20
  1092.4 56.6 reduce-scatter.16
  1152.8 64.2 reduce-scatter.36
  1220.8 64.2 reduce-scatter.32
  1288.9 64.1 reduce-scatter.40
where the time goes:
time: 1370 us; the launch traced here: 1360 us
  waiting for transfers between devices  1030 us (75%)
  local copies, waits for them, and re-layouts  89.7 us (7%)
  blocking collectives  79 us (6%)
  matrix products  76.4 us (6%)
  other arithmetic  40.7 us (3%)
  starting transfers between devices  33.1 us (2%)
  between operations  16.7 us (1%)
    unnamed x3, blocking collectives  79 us
    reduce_scatter x1, waiting for transfers between devices, per_device(): lax.psum_scatter(seq_major(grad_wg, outer, groups).astype(jnp.bfloat16),...  73.7 us
    reduce_scatter x1, waiting for transfers between devices, per_device(): lax.psum_scatter(seq_major(grad_wu, outer, groups).astype(jnp.bfloat16),...  73.6 us
    reduce_scatter x1, waiting for transfers between devices, per_device(): lax.psum_scatter(seq_major(grad_wd, outer, groups).astype(jnp.bfloat16),...  73.6 us
    reduce_scatter x1, waiting for transfers between devices, per_device(): lax.psum_scatter(ffn_part[2].astype(jnp.bfloat16), 'dp', scatter_dimensio...  66.6 us
    all_gather x1, waiting for transfers between devices, per_device(): lax.all_gather(w_gate, ('dp', 'seq'), axis=0, tiled=True)  66.5 us
    reduce_scatter x1, waiting for transfers between devices, per_device(): lax.psum_scatter(ffn_part[3].astype(jnp.bfloat16), 'dp', scatter_dimensio...  66.3 us
    reduce_scatter x1, waiting for transfers between devices, per_device(): lax.psum_scatter(ffn_part[1].astype(jnp.bfloat16), 'dp', scatter_dimensio...  66.3 us
  transfers between devices with their start and end apart: 29, of which 25 were waited for; matrix products, arithmetic and copies ran while one was open for 13% of the time, Pallas kernels for 0%

commit v1 on v0

--- a/solution.py
+++ b/solution.py
@@ -1,6 +1,10 @@
+import functools
+
 import jax
 import jax.numpy as jnp
 from jax import lax
+from jax.experimental import pallas as pl
+from jax.experimental.pallas import tpu as pltpu
 from jax.sharding import PartitionSpec as P
 
 H = 16
@@ -356,7 +360,437 @@
     )
 
 
+MESH = pl.DeviceIdType.MESH
+CHIPS = 8
+BF = jnp.bfloat16
+F32 = jnp.float32
+
+
+def place():
+    x = lax.axis_index("seq")
+    dp = lax.axis_index("dp")
+    core = lax.rem(dp, 2)
+    chip = lax.div(dp, 2)
+    y = lax.rem(chip, 2)
+    z = lax.div(chip, 2)
+    pos = z * (1 - y) + (CHIPS - 1 - z) * y
+    return x, dp, core, chip, pos
+
+
+def chip_at(pos):
+    pos = lax.rem(pos + 2 * CHIPS, CHIPS)
+    half = CHIPS // 2
+    y = lax.div(pos, half)
+    z = pos * (1 - y) + (CHIPS - 1 - pos) * y
+    return 2 * z + y
+
+
+def greet(peers):
+    bar = pltpu.get_barrier_semaphore()
+    for peer in peers:
+        pl.semaphore_signal(bar, inc=1, device_id=peer, device_id_type=MESH)
+    pl.semaphore_wait(bar, len(peers))
+
+
+COLS = (0, 1, 2, 3)
+ROWS = (4, 5)
+
+
+def block_of(buf, t, chip, core, way):
+    if t in COLS:
+        return buf.at[2 * chip + core, way]
+    return buf.at[chip, core, way]
+
+
+def gather_kernel(*refs):
+    ins = refs[0:6]
+    bufs = refs[6:12]
+    ring_s, ring_r, mate_s, mate_r, swap_s, swap_r, local = refs[12:]
+    x, dp, core, chip, pos = place()
+    right = (2 * chip_at(pos + 1) + core, x)
+    left = (2 * chip_at(pos - 1) + core, x)
+    mate = (2 * chip + 1 - core, x)
+    across = (dp, 1 - x)
+    diagonal = (2 * chip + 1 - core, 1 - x)
+    greet((right, left, mate, across, diagonal))
+
+    def swap(t):
+        if t == 0:
+            src, dst, to = ins[t], bufs[t].at[dp, x], across
+        elif t in COLS:
+            src, dst, to = ins[t].at[1 - x], bufs[t].at[dp, x], across
+        else:
+            src, dst, to = ins[t], bufs[t].at[chip, x], diagonal
+        return pltpu.make_async_remote_copy(
+            src_ref=src, dst_ref=dst, send_sem=swap_s.at[t], recv_sem=swap_r.at[t],
+            device_id=to, device_id_type=MESH)
+
+    def keep(t):
+        if t == 0:
+            src, dst = ins[t], bufs[t].at[dp, x]
+        elif t in COLS:
+            src, dst = ins[t].at[x], bufs[t].at[dp, x]
+        else:
+            src, dst = ins[t], bufs[t].at[chip, x]
+        return pltpu.make_async_copy(src, dst, local.at[t])
+
+    def hop(t, step, way):
+        origin = chip_at(pos - step) if way == 0 else chip_at(pos + step)
+        block = block_of(bufs[t], t, origin, core, way)
+        return pltpu.make_async_remote_copy(
+            src_ref=block, dst_ref=block, send_sem=ring_s.at[t, step, way],
+            recv_sem=ring_r.at[t, step, way], device_id=right if way == 0 else left,
+            device_id_type=MESH)
+
+    def share(t, step, way):
+        origin = chip_at(pos - step) if way == 0 else chip_at(pos + step)
+        block = block_of(bufs[t], t, origin, core, way)
+        return pltpu.make_async_remote_copy(
+            src_ref=block, dst_ref=block, send_sem=mate_s.at[t, step, way],
+            recv_sem=mate_r.at[t, step, way], device_id=mate, device_id_type=MESH)
+
+    for t in COLS:
+        swap(t).start()
+        keep(t).start()
+    for t in ROWS:
+        @pl.when(core != x)
+        def _():
+            swap(t).start()
+
+        @pl.when(core == x)
+        def _():
+            keep(t).start()
+    for t in COLS:
+        keep(t).wait()
+        swap(t).wait()
+    for t in ROWS:
+        @pl.when(core != x)
+        def _():
+            swap(t).wait()
+
+        @pl.when(core == x)
+        def _():
+            keep(t).wait()
+    for step in range(CHIPS):
+        for t in COLS + ROWS:
+            for way in (0, 1):
+                if step > 0:
+                    hop(t, step - 1, way).wait_recv()
+                if step < CHIPS - 1:
+                    hop(t, step, way).start()
+                share(t, step, way).start()
+    for step in range(CHIPS):
+        for t in COLS + ROWS:
+            for way in (0, 1):
+                if step < CHIPS - 1:
+                    hop(t, step, way).wait_send()
+                share(t, step, way).wait()
+
+
+def gather_weights(ins):
+    gains, qkv, gate, up, out, down = ins
+    shapes = [(2 * CHIPS, 2) + gains.shape]
+    for w in (qkv, gate, up):
+        shapes.append((2 * CHIPS, 2) + w.shape[1:])
+    shapes.append((CHIPS, 2) + out.shape)
+    shapes.append((CHIPS, 2) + down.shape)
+    anywhere = pl.BlockSpec(memory_space=pl.ANY)
+    return pl.pallas_call(
+        gather_kernel,
+        out_shape=[jax.ShapeDtypeStruct(s, BF) for s in shapes],
+        in_specs=[anywhere] * 6,
+        out_specs=[anywhere] * 6,
+        scratch_shapes=[pltpu.SemaphoreType.DMA((6, CHIPS, 2))] * 4
+        + [pltpu.SemaphoreType.DMA((6,))] * 3,
+        compiler_params=pltpu.CompilerParams(collective_id=0, has_side_effects=True),
+    )(*ins)
+
+
+def scatter_kernel(*refs):
+    parts = refs[0:6]
+    outs = refs[6:12]
+    own = refs[12:18]
+    from_mate = refs[18:24]
+    landing = refs[24:30]
+    swapped = refs[30:36]
+    ring_s, ring_r, mate_s, mate_r, swap_s, swap_r, local = refs[36:]
+    x, dp, core, chip, pos = place()
+    right = (2 * chip_at(pos + 1) + core, x)
+    left = (2 * chip_at(pos - 1) + core, x)
+    mate = (2 * chip + 1 - core, x)
+    across = (dp, 1 - x)
+    diagonal = (2 * chip + 1 - core, 1 - x)
+
+    def load(t):
+        return pltpu.make_async_copy(parts[t].at[:, core], own[t], local.at[t])
+
+    def share(t):
+        return pltpu.make_async_remote_copy(
+            src_ref=parts[t].at[:, 1 - core], dst_ref=from_mate[t], send_sem=mate_s.at[t],
+            recv_sem=mate_r.at[t], device_id=mate, device_id_type=MESH)
+
+    def hop(t, step, way):
+        dest = chip_at(pos - 1 - step) if way == 0 else chip_at(pos + 1 + step)
+        return pltpu.make_async_remote_copy(
+            src_ref=own[t].at[dest, way], dst_ref=landing[t].at[step, way],
+            send_sem=ring_s.at[t, step, way], recv_sem=ring_r.at[t, step, way],
+            device_id=right if way == 0 else left, device_id_type=MESH)
+
+    def swap(t):
+        if t in COLS:
+            return pltpu.make_async_remote_copy(
+                src_ref=own[t].at[chip, 1 - x], dst_ref=swapped[t], send_sem=swap_s.at[t],
+                recv_sem=swap_r.at[t], device_id=across, device_id_type=MESH)
+        return pltpu.make_async_remote_copy(
+            src_ref=own[t].at[chip], dst_ref=swapped[t], send_sem=swap_s.at[t],
+            recv_sem=swap_r.at[t], device_id=diagonal, device_id_type=MESH)
+
+    order = ROWS + COLS
+    for t in order:
+        load(t).start()
+    greet((right, left, mate, across, diagonal))
+    for t in order:
+        share(t).start()
+    for t in order:
+        load(t).wait()
+        share(t).wait_recv()
+        for step in range(CHIPS):
+            for way in (0, 1):
+                dest = chip_at(pos - 1 - step) if way == 0 else chip_at(pos + 1 + step)
+                mine = own[t][dest, way].astype(F32) + from_mate[t][dest, way].astype(F32)
+                own[t][dest, way] = mine.astype(own[t].dtype)
+                if step == 0:
+                    hop(t, 0, way).start()
+    for step in range(1, CHIPS):
+        for t in order:
+            for way in (0, 1):
+                hop(t, step - 1, way).wait_recv()
+                dest = chip_at(pos - 1 - step) if way == 0 else chip_at(pos + 1 + step)
+                mine = own[t][dest, way].astype(F32) + landing[t][step - 1, way].astype(F32)
+                own[t][dest, way] = mine.astype(own[t].dtype)
+                if step < CHIPS - 1:
+                    hop(t, step, way).start()
+    for t in COLS:
+        swap(t).start()
+    for t in ROWS:
+        @pl.when(core != x)
+        def _():
+            swap(t).start()
+    for t in COLS:
+        swap(t).wait()
+        mine = own[t][chip, x].astype(F32)
+        other = swapped[t][...].astype(F32)
+        if t == 0:
+            outs[t][...] = mine + other
+        else:
+            outs[t][x] = mine
+            outs[t][1 - x] = other
+    for t in ROWS:
+        @pl.when(core != x)
+        def _():
+            swap(t).wait()
+            outs[t][...] = swapped[t][...].astype(F32)
+
+        @pl.when(core == x)
+        def _():
+            outs[t][...] = own[t][chip].astype(F32)
+    for t in order:
+        share(t).wait_send()
+        for step in range(CHIPS - 1):
+            for way in (0, 1):
+                hop(t, step, way).wait_send()
+
+
+def scatter_grads(parts):
+    anywhere = pl.BlockSpec(memory_space=pl.ANY)
+    inner = [p.shape[3:] for p in parts]
+    kinds = [p.dtype for p in parts]
+    outs, swaps = [], []
+    for t in range(6):
+        if t == 0:
+            outs.append(inner[t])
+            swaps.append(inner[t])
+        elif t in COLS:
+            outs.append((2,) + inner[t])
+            swaps.append(inner[t])
+        else:
+            outs.append((2,) + inner[t])
+            swaps.append((2,) + inner[t])
+    return pl.pallas_call(
+        scatter_kernel,
+        out_shape=[jax.ShapeDtypeStruct(s, F32) for s in outs],
+        in_specs=[anywhere] * 6,
+        out_specs=[pl.BlockSpec(memory_space=pltpu.VMEM)] * 6,
+        scratch_shapes=[pltpu.VMEM((CHIPS, 2) + s, d) for s, d in zip(inner, kinds)]
+        + [pltpu.VMEM((CHIPS, 2) + s, d) for s, d in zip(inner, kinds)]
+        + [pltpu.VMEM((CHIPS - 1, 2) + s, d) for s, d in zip(inner, kinds)]
+        + [pltpu.VMEM(s, d) for s, d in zip(swaps, kinds)]
+        + [pltpu.SemaphoreType.DMA((6, CHIPS, 2))] * 2
+        + [pltpu.SemaphoreType.DMA((6,))] * 5,
+        compiler_params=pltpu.CompilerParams(
+            collective_id=1, has_side_effects=True, vmem_limit_bytes=60 * 2**20),
+    )(*parts)
+
+
+def by_parity(w, groups, unit):
+    return w.reshape(w.shape[0], groups, 2, unit).transpose(2, 0, 1, 3).reshape(
+        2, w.shape[0], groups * unit)
+
+
+def from_parity(w, groups, unit):
+    return w.reshape(2, w.shape[1], groups, unit).transpose(1, 2, 0, 3).reshape(
+        w.shape[1], groups * 2 * unit)
+
+
+def per_pair(
+    tokens, first_values, doc_ids, cotangent, norm1_gain, w_query, w_key, w_value, w_out,
+    norm2_gain, w_gate, w_up, w_down,
+):
+    x = lax.axis_index("seq")
+    dp = lax.axis_index("dp")
+    rows, width = tokens.shape[1:]
+    stream = 2 * rows
+    head = width // H
+    heads = H // 2
+    flat = heads * head
+    units = w_gate.shape[1] // 2
+    unit = units // CHIPS
+    share = norm1_gain.shape[0]
+
+    def flip(t):
+        return lax.ppermute(t, "seq", [(0, 1), (1, 0)])
+
+    def both(t):
+        other = flip(t)
+        pair = jnp.stack([t, other])
+        return jnp.where(x == 0, pair, pair[::-1]).reshape((2 * t.shape[0],) + t.shape[1:])
+
+    def mine(t):
+        return lax.dynamic_slice_in_dim(t, x * rows, rows, 0)
+
+    def theirs(t):
+        return lax.dynamic_slice_in_dim(t, (1 - x) * rows, rows, 0)
+
+    def summed(t):
+        return mine(t) + flip(theirs(t).astype(BF)).astype(F32)
+
+    lanes = 128
+    per_tile = lanes // share
+    seat = lax.rem(2 * dp + x, per_tile)
+    lane = lax.broadcasted_iota(jnp.int32, (1, lanes), 1)
+
+    def seated(g):
+        return jnp.where(lane // share == seat, jnp.tile(g, per_tile)[None], 0).astype(BF)
+
+    tile = jnp.concatenate([seated(norm1_gain), seated(norm2_gain), jnp.zeros((6, lanes), BF)])
+    qkv_in = jnp.concatenate([by_parity(w, heads, head) for w in (w_query, w_key, w_value)], axis=2)
+    half = w_out.shape[0] // 2
+    out_in = w_out.reshape(2, half, width)
+    down_in = w_down.reshape(w_down.shape[0], 2, width // 2).transpose(1, 0, 2)
+    gains, wqkv, wg, wu, wo, wd = gather_weights(
+        (tile, qkv_in, by_parity(w_gate, CHIPS, unit), by_parity(w_up, CHIPS, unit), out_in, down_in))
+    gains = gains.reshape(width // lanes, per_tile, 8, lanes).astype(F32).sum(1)
+    gain1 = gains[:, 0].reshape(width)
+    gain2 = gains[:, 1].reshape(width)
+    wqkv = wqkv.reshape(width, 3 * flat)
+    wg = wg.reshape(width, units)
+    wu = wu.reshape(width, units)
+    wo = wo.reshape(flat, width)
+    wd = wd.transpose(0, 1, 3, 2, 4).reshape(units, width)
+
+    tok = both(tokens[0])
+    x_all = tok.astype(F32)
+    normed1, inverse1 = norm_forward(x_all, gain1)
+    n1 = normed1.astype(BF)
+    qkv = jnp.dot(n1, wqkv, preferred_element_type=F32).reshape(stream, 3, heads, head)
+    cos_tab, sin_tab = rope_tables(0, stream, head)
+    query = rotate(qkv[:, 0], cos_tab, sin_tab, 1.0).astype(BF)
+    key = rotate(qkv[:, 1], cos_tab, sin_tab, 1.0).astype(BF)
+    first2 = by_parity(first_values[0], heads, head)
+    first_mine = lax.dynamic_index_in_dim(first2, x, 0, keepdims=False)
+    first_theirs = flip(lax.dynamic_index_in_dim(first2, 1 - x, 0, keepdims=False))
+    pair = jnp.stack([first_mine, first_theirs])
+    first = jnp.where(x == 0, pair, pair[::-1]).reshape(stream, heads, head)
+    value = (0.5 * (qkv[:, 2] + first.astype(F32))).astype(BF)
+    segment = doc_ids[0]
+    positions = jnp.arange(stream, dtype=jnp.int32)
+    mask = (segment[:, None] == segment[None, :]) & (positions[None, :] <= positions[:, None])
+    scale = head ** (-0.5)
+    scores = jnp.einsum("qhd,khd->hqk", query, key, preferred_element_type=F32) * scale
+    scores = jnp.where(mask[None], scores, -1e30)
+    peak = jnp.max(scores, axis=-1, keepdims=True)
+    expo = jnp.exp(scores - peak)
+    probs = expo / jnp.sum(expo, axis=-1, keepdims=True)
+    probs_b = probs.astype(BF)
+    mixed = jnp.einsum("hqk,khd->qhd", probs_b, value, preferred_element_type=F32).astype(BF)
+    mixed = mixed.reshape(stream, flat)
+    h1 = mine(x_all) + summed(jnp.dot(mixed, wo, preferred_element_type=F32))
+    normed2, inverse2 = norm_forward(h1, gain2)
+    n2 = both(normed2.astype(BF))
+    gate = jnp.dot(n2, wg, preferred_element_type=F32)
+    up = jnp.dot(n2, wu, preferred_element_type=F32)
+    sigma = jax.nn.sigmoid(gate)
+    active = gate * sigma
+    hidden = (active * up).astype(BF)
+    layer_out = (h1 + summed(jnp.dot(hidden, wd, preferred_element_type=F32))).astype(BF)[None]
+    dy = both(cotangent[0])
+    grad_wd = matmul_left(hidden, dy).astype(BF)
+    g_hidden = matmul_right(dy, wd)
+    g_gate = (g_hidden * up * sigma * (1.0 + gate * (1.0 - sigma))).astype(BF)
+    g_up = (g_hidden * active).astype(BF)
+    grad_wg = matmul_left(n2, g_gate).astype(BF)
+    grad_wu = matmul_left(n2, g_up).astype(BF)
+    g_n2 = summed(matmul_right(g_gate, wg) + matmul_right(g_up, wu))
+    g_h1_norm, grad_g2 = norm_backward(h1, inverse2, gain2, g_n2)
+    g_h1 = mine(dy).astype(F32) + g_h1_norm
+    g_att = both(g_h1.astype(BF))
+    grad_wo = matmul_left(mixed, g_att).astype(BF)
+    g_mixed = matmul_right(g_att, wo).astype(BF).reshape(stream, heads, head)
+    g_probs = jnp.einsum("qhd,khd->hqk", g_mixed, value, preferred_element_type=F32)
+    delta = jnp.sum(probs * g_probs, axis=-1, keepdims=True)
+    g_scores = (probs * (g_probs - delta)).astype(BF)
+    g_query = (jnp.einsum("hqk,khd->qhd", g_scores, key, preferred_element_type=F32) * scale)
+    g_key = (jnp.einsum("hqk,qhd->khd", g_scores, query, preferred_element_type=F32) * scale)
+    g_value = jnp.einsum("hqk,qhd->khd", probs_b, g_mixed, preferred_element_type=F32)
+
+    def unrotate(t):
+        t = t.astype(BF).astype(F32)
+        return rotate(t, cos_tab, sin_tab, -1.0).astype(BF).reshape(stream, flat)
+
+    g_vlin = (0.5 * g_value).astype(BF).reshape(stream, flat)
+    g_lin = jnp.concatenate([unrotate(g_query), unrotate(g_key), g_vlin], axis=1)
+    grad_wqkv = matmul_left(n1, g_lin).astype(BF)
+    g_n1 = summed(matmul_right(g_lin, wqkv))
+    g_x, grad_g1 = norm_backward(mine(x_all), mine(inverse1), gain1, g_n1)
+    grad_tokens = (g_h1 + g_x).astype(BF)[None]
+    gv_mine = mine(g_vlin)
+    gv_theirs = flip(theirs(g_vlin))
+    pair = jnp.stack([gv_mine, gv_theirs])
+    grad_first = from_parity(jnp.where(x == 0, pair, pair[::-1]), heads, head)[None]
+
+    chunks = jnp.stack([grad_g1, grad_g2]).reshape(2, width // lanes, lanes).transpose(1, 0, 2)
+    chunks = jnp.pad(chunks, ((0, 0), (0, 6), (0, 0)))
+    gain_parts = jnp.repeat(chunks, per_tile, axis=0)
+    devs = 2 * CHIPS
+    out = scatter_grads((
+        gain_parts.reshape(CHIPS, 2, 2, 8, lanes),
+        grad_wqkv.reshape(CHIPS, 2, 2, share, 3 * flat),
+        grad_wg.reshape(CHIPS, 2, 2, share, units),
+        grad_wu.reshape(CHIPS, 2, 2, share, units),
+        grad_wo.reshape(CHIPS, 2, 2, half, width),
+        grad_wd.reshape(CHIPS, 2, w_down.shape[0], 2, width // 2).transpose(0, 1, 3, 2, 4),
+    ))
+    g12 = lax.dynamic_slice_in_dim(out[0], seat * share, share, 1)
+    gq, gk, gv = [from_parity(out[1][:, :, i * flat:(i + 1) * flat], heads, head) for i in range(3)]
+    return (
+        layer_out, grad_tokens, grad_first, g12[0], gq, gk, gv, out[4].reshape(2 * half, width),
+        g12[1], from_parity(out[2], CHIPS, unit), from_parity(out[3], CHIPS, unit),
+        out[5].transpose(1, 0, 2).reshape(w_down.shape[0], width),
+    )
+
+
 def solution(mesh):
+    on_ring = mesh.shape["dp"] == 2 * CHIPS and mesh.shape["seq"] == 2
     placed = (
         P("dp", "seq", None),
         P("dp", "seq", None),
@@ -373,22 +807,9 @@
         P(("dp", "seq"), None),
     )
     return jax.shard_map(
-        per_device,
+        per_pair if on_ring else per_device,
         mesh=mesh,
         in_specs=placed,
-        out_specs=(
-            P("dp", "seq", None),
-            P("dp", "seq", None),
-            P("dp", "seq", None),
-            P(("dp", "seq")),
-            P(("dp", "seq"), None),
-            P(("dp", "seq"), None),
-            P(("dp", "seq"), None),
-            P(("dp", "seq"), None),
-            P(("dp", "seq")),
-            P(("dp", "seq"), None),
-            P(("dp", "seq"), None),
-            P(("dp", "seq"), None),
-        ),
+        out_specs=placed[:2] + placed[3:],
         check_vma=False,
     )

time: 1370 us -> 378 us (0.28)
  the two profiles are of different devices: /device:TPU:0 before, /device:TPU:1 now
where the time goes in v1:
time: 378 us; the launch traced here: 372 us
  Pallas kernels  182 us (48%)
  local copies, waits for them, and re-layouts  62.2 us (16%)
  matrix products  51.1 us (14%)
  waiting for transfers between devices  40.1 us (11%)
  other arithmetic  26.7 us (7%)
  starting transfers between devices  7.67 us (2%)
    pallas_call x1, Pallas kernels, gather_weights(): pl.pallas_call(gather_kernel, out_shape=[jax.ShapeDtypeStruct(s, BF) for...  96.7 us
    pallas_call x1, Pallas kernels, scatter_grads(): pl.pallas_call(scatter_kernel, out_shape=[jax.ShapeDtypeStruct(s, F32) fo...  85.7 us
    ppermute x10, waiting for transfers between devices, flip(): return lax.ppermute(t, 'seq', [(0, 1), (1, 0)])  40.1 us
    dot_general x5, matrix products, matmul_left(): lax.dot_general(a, b, (((0,), (0,)), ((), ())), preferred_element_type=jn...  16.9 us
    reshape x2, local copies, waits for them, and re-layouts, per_pair(): grad_wd.reshape(CHIPS, 2, w_down.shape[0], 2, width // 2)  12 us
    unnamed x100, local copies, waits for them, and re-layouts  11.8 us
    reshape x10, local copies, waits for them, and re-layouts, from_parity(): w.reshape(2, w.shape[1], groups, unit).transpose(1, 2, 0, 3)  11.3 us
    dot_general x5, matrix products, matmul_right(): lax.dot_general(a, b, (((1,), (1,)), ((), ())), preferred_element_type=jn...  9.54 us
  transfers between devices with their start and end apart: 10, of which 5 were waited for; matrix products, arithmetic and copies ran while one was open for 21% of the time, Pallas kernels for 26%

profile of v1, /device:TPU:1, one launch (start us, length us, event | category | flops | bytes accessed | tf_op | source)
XLA Modules:
  0.0 372.3 jit_solution(8489199384164639038)
XLA Ops:
  0.7 1.3 copy.96
  2.2 2.1 collective-permute-start.1
  4.3 1.4 collective-permute-start.5
  12.0 96.7 %shard_map.220 = (bf16[16,2,8,128]{3,2,1,0:T(8,128)(2,1)}, bf16[16,2,32,1536]{3,2,1,0:T(8,128)(2,1)}, bf16[16,2,32,1408]{3,2,1,0:T(8,128)(2,1)}, bf16[16,2,32,14...) custom-call(bf16[8,128]{1,0:T(8,128)(2,1)} %maximum_maximum_fusion.refs_0_, ...), custom_call_target="tpu_custom_call" | custom-call | tf_op jit(solution)/shard_map/pallas_call | solution.py:498
  111.4 4.9 %copy.95 = bf16[1536,1024]{1,0:T(8,128)(2,1)} copy(bf16[1536,1024]{0,1:T(8,128)(2,1)} %bitcast.186) | data formatting | bytes 6291456 | tf_op jit(solution)/shard_map/dot_general | solution.py:705
  119.0 1.6 pad_maximum_fusion.1
  122.0 1.8 fusion.55
  125.5 6.9 %fusion.54 = (f32[8,512]{1,0:T(8,128)S(1)}, f32[8,512,512]{1,2,0:T(8,128)}) fusion(pred[512,512]{0,1:T(8,128)(4,1)} %fusion.31, bf16[512,8,32]{0,2,1:T(8,128)(2,1)S(1)} %get-tuple-element.103, bf16[512,8,32]{0,2,1:T(8,128)(2,1)S(1)} %get-tuple-element.104, bf16[512,8,32]{0,2,1:T(8,128)(2,1)S(1)} %get-tuple-element.90, ...), kind=kOutput, calls=%fused_computation.146 | convolution fusion | flops 278921728 | bytes 9715712 | tf_op jit(solution)/shard_map/sub | solution.py:722
  132.4 4.3 %fusion.13 = bf16[8,64,512]{2,1,0:T(8,128)(2,1)S(1)} fusion(bf16[512,8,64]{0,2,1:T(8,128)(2,1)S(1)} %copy-done.22, f32[8,512,512]{1,2,0:T(8,128)} %get-tuple-element.116, f32[8,512]{1,0:T(8,128)S(1)} %get-tuple-element.115), kind=kOutput, calls=%fused_computation.37 | convolution fusion | flops 272891904 | bytes 9453568 | tf_op jit(solution)/shard_map/hqk,khd->qhd/dot_general | solution.py:725
  140.4 1.6 reverse_select_fusion.1
  142.0 9.9 %collective-permute-done.2 = bf16[256,1024]{1,0:T(8,128)(2,1)} collective-permute-done((bf16[256,1024]{1,0:T(8,128)(2,1)}, bf16[256,1024]{1,0:T(8,128)(2,1)}, u32[]{:S(2)}, u32[]{:S(2)}) %collective-permute-start.2) | collective-permute-done | bytes 524320 | tf_op jit(solution)/shard_map/ppermute | solution.py:661
  151.9 1.3 multiply_reduce_fusion.6
  154.5 2.7 copy.100
  157.2 2.3 copy.120
  161.5 5.3 %collective-permute-done.3 = bf16[256,1024]{1,0:T(8,128)(2,1)} collective-permute-done((bf16[256,1024]{1,0:T(8,128)(2,1)}, bf16[256,1024]{1,0:T(8,128)(2,1)}, u32[]{:S(2)}, u32[]{:S(2)}) %collective-permute-start.3) | collective-permute-done | bytes 524320 | tf_op jit(solution)/shard_map/ppermute | solution.py:661
  168.2 1.8 fusion.57
  170.4 1.8 fusion.58
  172.5 3.3 multiply_convert_fusion.1
  175.8 1.8 fusion.60
  177.7 1.8 convolution_add_fusion
  180.2 1.8 fusion.59
  183.1 3.4 convolution_convert_fusion.2
  186.5 4.5 %collective-permute-done.6 = bf16[256,1024]{1,0:T(8,128)(2,1)S(1)} collective-permute-done((bf16[256,1024]{1,0:T(8,128)(2,1)S(1)}, bf16[256,1024]{1,0:T(8,128)(2,1)S(1)}, u32[]{:S(2)}, u32[]{:S(2)}) %collective-permute-start.6) | collective-permute-done | bytes 524320 | tf_op jit(solution)/shard_map/ppermute | solution.py:661
  191.5 10.8 %collective-permute-done.4 = bf16[256,1024]{1,0:T(8,128)(2,1)S(1)} collective-permute-done((bf16[256,1024]{1,0:T(8,128)(2,1)S(1)}, bf16[256,1024]{1,0:T(8,128)(2,1)S(1)}, u32[]{:S(2)}, u32[]{:S(2)}) %collective-permute-start.4) | collective-permute-done | bytes 524320 | tf_op jit(solution)/shard_map/ppermute | solution.py:661
  202.3 1.9 fusion.51
  205.0 3.3 convolution_convert_fusion
  208.2 7.9 %reshape.452 = bf16[8,2,88,2,512]{4,3,2,1,0:T(2,128)(2,1)} reshape(bf16[1408,1024]{1,0:T(8,128)(2,1)} %convolution_convert_fusion) | data formatting | bytes 5767168 | tf_op jit(solution)/shard_map/reshape | solution.py:781
  216.1 4.1 %copy.130 = bf16[8,2,88,2,512]{4,2,3,1,0:T(8,128)(2,1)} copy(bf16[8,2,88,2,512]{4,3,2,1,0:T(2,128)(2,1)} %reshape.452) | data formatting | bytes 5767168 | tf_op jit(solution)/shard_map/reshape | solution.py:781
  220.3 4.9 %convolution_convert_fusion.1 = bf16[1024,1408]{1,0:T(8,128)(2,1)} fusion(bf16[512,1024]{1,0:T(8,128)(2,1)S(1)} %bitcast.210, bf16[512,1408]{1,0:T(8,128)(2,1)} %copy-done.44), kind=kOutput, calls=%fused_computation.11 | convolution fusion | flops 1477836800 | bytes 5373952 | tf_op jit(solution)/shard_map/dot_general | solution.py:55
  227.5 1.4 fusion.22
  228.9 2.0 multiply_reduce_fusion
  230.9 2.8 multiply_convert_fusion
  234.7 1.4 fusion.21
  236.6 1.4 copy-done.4
  238.0 1.8 fusion.34
  239.9 1.3 copy-done.3
  243.5 3.7 convolution_convert_fusion.3
  247.2 1.7 convolution_convert_fusion.4
  248.9 9.5 %collective-permute-done.9 = bf16[256,512]{0,1:T(8,128)(2,1)S(1)} collective-permute-done((bf16[256,512]{0,1:T(8,128)(2,1)S(1)}, bf16[256,512]{0,1:T(8,128)(2,1)S(1)}, u32[]{:S(2)}, u32[]{:S(2)}) %collective-permute-start.9) | collective-permute-done | bytes 262176 | tf_op jit(solution)/shard_map/ppermute | solution.py:661
  259.6 1.8 multiply_reduce_fusion.3
  262.1 85.7 %shard_map.221 = (f32[8,128]{1,0:T(8,128)}, f32[2,32,1536]{2,1,0:T(8,128)}, f32[2,32,1408]{2,1,0:T(8,128)}, f32[2,32,1408]{2,1,0:T(8,128)}, f32[2,16,1024]{2,1,0:T(8,128)}, /*index=5*/f32[2,88,512]{2,1,0:T(8,128)}) custom-call(f32[8,2,2,8,128]{4,3,2,1,0:T(8,128)} %reshape_reshape.3.refs_0_, bf16[8,2,2,32,1536]{4,3,2,1,0:T(8,128)(2,1)} %bitcast.189, ...), custom_call_target="tpu_custom_call" | custom-call | tf_op jit(solution)/shard_map/pallas_call | solution.py:619
  353.9 2.2 reshape.460
  356.1 2.4 copy.109
  358.4 2.4 reshape.461
  362.0 2.3 copy.110
  364.3 2.5 reshape.463
  366.8 1.7 copy.119
  368.5 2.6 fusion.37
  (196 shorter events, 42.3 us)
Async XLA Ops:
  0.6 3.6 copy-start.24
  0.7 5.1 %copy-start.42 = (bf16[32]{0:T(256)(128)(2,1)S(1)}, bf16[32]{0:T(256)(128)(2,1)}, u32[]{:S(2)}) copy-start(bf16[32]{0:T(256)(128)(2,1)} %param.22) | copy-start | bytes 196
  0.7 5.2 %copy-start.43 = (bf16[32]{0:T(256)(128)(2,1)S(1)}, bf16[32]{0:T(256)(128)(2,1)}, u32[]{:S(2)}) copy-start(bf16[32]{0:T(256)(128)(2,1)} %param.17) | copy-start | bytes 196
  0.7 5.3 %copy-start.32 = (bf16[32,1024]{1,0:T(8,128)(2,1)S(1)}, bf16[32,1024]{1,0:T(8,128)(2,1)}, u32[]{:S(2)}) copy-start(bf16[32,1024]{1,0:T(8,128)(2,1)} %param.20) | copy-start | bytes 196612
  0.7 5.6 %copy-start.33 = (bf16[32,1024]{1,0:T(8,128)(2,1)S(1)}, bf16[32,1024]{1,0:T(8,128)(2,1)}, u32[]{:S(2)}) copy-start(bf16[32,1024]{1,0:T(8,128)(2,1)} %param.19) | copy-start | bytes 196612
  0.7 5.9 %copy-start.34 = (bf16[32,1024]{1,0:T(8,128)(2,1)S(1)}, bf16[32,1024]{1,0:T(8,128)(2,1)}, u32[]{:S(2)}) copy-start(bf16[32,1024]{1,0:T(8,128)(2,1)} %param.18) | copy-start | bytes 196612
  0.7 6.2 %copy-start.28 = (bf16[32,2816]{1,0:T(8,128)(2,1)S(1)}, bf16[32,2816]{1,0:T(8,128)(2,1)}, u32[]{:S(2)}) copy-start(bf16[32,2816]{1,0:T(8,128)(2,1)} %param.23) | copy-start | bytes 540676
  2.0 6.4 %copy-start.29 = (bf16[32,2816]{1,0:T(8,128)(2,1)S(1)}, bf16[32,2816]{1,0:T(8,128)(2,1)}, u32[]{:S(2)}) copy-start(bf16[32,2816]{1,0:T(8,128)(2,1)} %param.24) | copy-start | bytes 540676
  2.1 7.8 %copy-start.30 = (bf16[88,1024]{1,0:T(8,128)(2,1)S(1)}, bf16[88,1024]{1,0:T(8,128)(2,1)}, u32[]{:S(2)}) copy-start(bf16[88,1024]{1,0:T(8,128)(2,1)} %param.25) | copy-start | bytes 540676
  2.2 114.2 %collective-permute-start.1 = (bf16[256,512]{0,1:T(8,128)(2,1)S(1)}, bf16[256,512]{0,1:T(8,128)(2,1)S(1)}, u32[]{:S(2)}, u32[]{:S(2)}) collective-permute-start(bf16[256,512]{0,1:T(8,128)(2,1)S(1)} %get-tuple-element.97), channel_id=1, source_target_pairs={{0,1},{1,0},{2,3},{3,2},{4,5},{5,4},{6,7},{7,6},{8,9},{9,8},{10,11... | collective-permute-start | bytes 786440 | tf_op jit(solution)/shard_map/ppermute | solution.py:661
  4.3 114.0 %collective-permute-start = (bf16[256,1024]{1,0:T(8,128)(2,1)S(1)}, bf16[256,1024]{1,0:T(8,128)(2,1)S(1)}, u32[]{:S(2)}, u32[]{:S(2)}) collective-permute-start(bf16[256,1024]{1,0:T(8,128)(2,1)S(1)} %bitcast.232), channel_id=1, source_target_pairs={{0,1},{1,0},{2,3},{3,2},{4,5},{5,4},{6,7},{7,6},{8,9},{9,8},{10,11... | collective-permute-start | bytes 1572872 | tf_op jit(solution)/shard_map/ppermute | solution.py:661
  4.3 134.2 %collective-permute-start.5 = (bf16[256,1024]{1,0:T(8,128)(2,1)}, bf16[256,1024]{1,0:T(8,128)(2,1)}, u32[]{:S(2)}, u32[]{:S(2)}) collective-permute-start(bf16[256,1024]{1,0:T(8,128)(2,1)} %bitcast.38), channel_id=1, source_target_pairs={{0,1},{1,0},{2,3},{3,2},{4,5},{5,4},{6,7},{7,6},{8,9},{9,8},{10,11... | collective-permute-start | bytes 1572872 | tf_op jit(solution)/shard_map/ppermute | solution.py:661
  6.3 103.3 %copy-start.38 = (s32[1,512]{1,0:T(1,128)S(1)}, s32[1,512]{1,0:T(1,128)}, u32[]{:S(2)}) copy-start(s32[1,512]{1,0:T(1,128)} %param.15) | copy-start | bytes 6148
  118.2 3.8 %copy-start.5 = (bf16[1536,1024]{1,0:T(8,128)(2,1)S(1)}, bf16[1536,1024]{1,0:T(8,128)(2,1)}, u32[]{:S(2)}) copy-start(bf16[1536,1024]{1,0:T(8,128)(2,1)} %copy.95) | copy-start | bytes 9437188
  125.5 6.9 %copy-start.12 = (bf16[512,8,32]{0,2,1:T(8,128)(2,1)}, bf16[512,8,32]{0,2,1:T(8,128)(2,1)S(1)}, u32[]{:S(2)}) copy-start(bf16[512,8,32]{0,2,1:T(8,128)(2,1)S(1)} %get-tuple-element.90) | copy-start | bytes 786436
  125.5 6.9 %copy-start.14 = (bf16[512,8,32]{0,2,1:T(8,128)(2,1)}, bf16[512,8,32]{0,2,1:T(8,128)(2,1)S(1)}, u32[]{:S(2)}) copy-start(bf16[512,8,32]{0,2,1:T(8,128)(2,1)S(1)} %get-tuple-element.103) | copy-start | bytes 786436
  125.5 6.9 %copy-start.16 = (bf16[512,8,32]{0,2,1:T(8,128)(2,1)}, bf16[512,8,32]{0,2,1:T(8,128)(2,1)S(1)}, u32[]{:S(2)}) copy-start(bf16[512,8,32]{0,2,1:T(8,128)(2,1)S(1)} %get-tuple-element.104) | copy-start | bytes 786436
  125.5 6.9 %copy-start.22 = (bf16[512,8,64]{0,2,1:T(8,128)(2,1)S(1)}, bf16[512,8,64]{0,2,1:T(8,128)(2,1)}, u32[]{:S(2)}) copy-start(bf16[512,8,64]{0,2,1:T(8,128)(2,1)} %fusion.28) | copy-start | bytes 1572868
  132.4 4.4 %copy-start.35 = (f32[8,512]{1,0:T(8,128)}, f32[8,512]{1,0:T(8,128)S(1)}, u32[]{:S(2)}) copy-start(f32[8,512]{1,0:T(8,128)S(1)} %get-tuple-element.115) | copy-start | bytes 49156
  132.4 4.4 %copy-start.10 = (bf16[8,2,2,16,1024]{4,3,2,1,0:T(8,128)(2,1)S(1)}, bf16[8,2,2,16,1024]{4,3,2,1,0:T(8,128)(2,1)}, u32[]{:S(2)}) copy-start(bf16[8,2,2,16,1024]{4,3,2,1,0:T(8,128)(2,1)} %get-tuple-element.26) | copy-start | bytes 3145732
  138.5 13.4 %collective-permute-start.2 = (bf16[256,1024]{1,0:T(8,128)(2,1)}, bf16[256,1024]{1,0:T(8,128)(2,1)}, u32[]{:S(2)}, u32[]{:S(2)}) collective-permute-start(bf16[256,1024]{1,0:T(8,128)(2,1)} %dynamic-slice_convert_fusion.3), channel_id=1, source_target_pairs={{0,1},{1,0},{2,3},{3,2},{4,5},{5,4},{6,7},{7,6},{8,9},{9,8},{10,11... | collective-permute-start | bytes 1572872 | tf_op jit(solution)/shard_map/ppermute | solution.py:661
  140.4 11.5 %copy-start.1 = (f32[512,1024]{1,0:T(8,128)S(1)}, f32[512,1024]{1,0:T(8,128)}, u32[]{:S(2)}) copy-start(f32[512,1024]{1,0:T(8,128)} %copy-done) | copy-start | bytes 6291460
  142.0 12.5 %copy-start.6 = (bf16[8,2,2,88,512]{4,3,2,1,0:T(8,128)(2,1)S(1)}, bf16[8,2,2,88,512]{4,3,2,1,0:T(8,128)(2,1)}, u32[]{:S(2)}) copy-start(bf16[8,2,2,88,512]{4,3,2,1,0:T(8,128)(2,1)} %get-tuple-element.29) | copy-start | bytes 8650756
  154.2 12.6 %collective-permute-start.3 = (bf16[256,1024]{1,0:T(8,128)(2,1)}, bf16[256,1024]{1,0:T(8,128)(2,1)}, u32[]{:S(2)}, u32[]{:S(2)}) collective-permute-start(bf16[256,1024]{1,0:T(8,128)(2,1)} %multiply_convert_fusion.7), channel_id=1, source_target_pairs={{0,1},{1,0},{2,3},{3,2},{4,5},{5,4},{6,7},{7,6},{8,9},{9,8},{10,11... | collective-permute-start | bytes 1572872 | tf_op jit(solution)/shard_map/ppermute | solution.py:661
  161.3 6.9 %copy-start.41 = (bf16[16,2,32,1408]{3,2,1,0:T(8,128)(2,1)S(1)}, bf16[16,2,32,1408]{3,2,1,0:T(8,128)(2,1)}, u32[]{:S(2)}) copy-start(bf16[16,2,32,1408]{3,2,1,0:T(8,128)(2,1)} %get-tuple-element.27) | copy-start | bytes 8650756
  168.2 14.9 %copy-start.18 = (bf16[2,256,1024]{2,1,0:T(8,128)(2,1)}, bf16[2,256,1024]{2,1,0:T(8,128)(2,1)S(1)}, u32[]{:S(2)}) copy-start(bf16[2,256,1024]{2,1,0:T(8,128)(2,1)S(1)} %reverse_select_fusion.2) | copy-start | bytes 3145732
  168.2 2.2 copy-start.40
  170.4 1.8 copy-start.7
  170.4 2.1 copy-start.8
  175.8 1.8 copy-start.44
  179.6 11.5 %collective-permute-start.6 = (bf16[256,1024]{1,0:T(8,128)(2,1)S(1)}, bf16[256,1024]{1,0:T(8,128)(2,1)S(1)}, u32[]{:S(2)}, u32[]{:S(2)}) collective-permute-start(bf16[256,1024]{1,0:T(8,128)(2,1)S(1)} %dynamic-slice_convert_fusion.1), channel_id=1, source_target_pairs={{0,1},{1,0},{2,3},{3,2},{4,5},{5,4},{6,7},{7,6},{8,9},{9,8},{10,11... | collective-permute-start | bytes 1572872 | tf_op jit(solution)/shard_map/ppermute | solution.py:661
  182.1 20.2 %collective-permute-start.4 = (bf16[256,1024]{1,0:T(8,128)(2,1)S(1)}, bf16[256,1024]{1,0:T(8,128)(2,1)S(1)}, u32[]{:S(2)}, u32[]{:S(2)}) collective-permute-start(bf16[256,1024]{1,0:T(8,128)(2,1)S(1)} %dynamic-slice_convert_fusion.2), channel_id=1, source_target_pairs={{0,1},{1,0},{2,3},{3,2},{4,5},{5,4},{6,7},{7,6},{8,9},{9,8},{10,11... | collective-permute-start | bytes 1572872 | tf_op jit(solution)/shard_map/ppermute | solution.py:661
  204.2 21.0 %collective-permute-start.7 = (bf16[256,1024]{1,0:T(8,128)(2,1)}, bf16[256,1024]{1,0:T(8,128)(2,1)S(1)}, u32[]{:S(2)}, u32[]{:S(2)}) collective-permute-start(bf16[256,1024]{1,0:T(8,128)(2,1)} %get-tuple-element.76), channel_id=1, source_target_pairs={{0,1},{1,0},{2,3},{3,2},{4,5},{5,4},{6,7},{7,6},{8,9},{9,8},{10,11... | collective-permute-start | bytes 1572872 | tf_op jit(solution)/shard_map/ppermute | solution.py:661
  216.1 4.2 %copy-start.19 = (bf16[2,256,1024]{2,1,0:T(8,128)(2,1)S(1)}, bf16[2,256,1024]{2,1,0:T(8,128)(2,1)}, u32[]{:S(2)}) copy-start(bf16[2,256,1024]{2,1,0:T(8,128)(2,1)} %copy-done.18) | copy-start | bytes 3145732
  216.1 11.3 %slice-start = ((s8[8388608]{0:T(1024)(128)(4,1)}), s8[4194304]{0:T(1024)(128)(4,1)S(1)}, s32[]{:S(2)}) async-start(s8[8388608]{0:T(1024)(128)(4,1)} %bitcast.184), calls=%async_computation | async-start | bytes 8388608
  220.3 7.2 %slice-start.1 = ((s8[8388608]{0:T(1024)(128)(4,1)}), s8[4194304]{0:T(1024)(128)(4,1)S(1)}, s32[]{:S(2)}) async-start(s8[8388608]{0:T(1024)(128)(4,1)} %bitcast.184), calls=%async_computation.1 | async-start | bytes 8388608
  230.9 2.8 copy-start.15
  230.9 2.8 copy-start.17
  236.1 1.9 copy-start.4
  238.0 5.5 %copy-start.39 = (f32[1,2,2,128]{3,1,2,0:T(2,128)S(1)}, f32[1,2,2,128]{3,1,2,0:T(2,128)}, u32[]{:S(2)}) copy-start(f32[1,2,2,128]{3,1,2,0:T(2,128)} %copy.122) | copy-start | bytes 6148
  242.1 17.6 %collective-permute-start.8 = (bf16[256,1024]{1,0:T(8,128)(2,1)}, bf16[256,1024]{1,0:T(8,128)(2,1)S(1)}, u32[]{:S(2)}, u32[]{:S(2)}) collective-permute-start(bf16[256,1024]{1,0:T(8,128)(2,1)} %dynamic-slice_convert_fusion), channel_id=1, source_target_pairs={{0,1},{1,0},{2,3},{3,2},{4,5},{5,4},{6,7},{7,6},{8,9},{9,8},{10,11... | collective-permute-start | bytes 1572872 | tf_op jit(solution)/shard_map/ppermute | solution.py:661
  242.8 15.7 %collective-permute-start.9 = (bf16[256,512]{0,1:T(8,128)(2,1)S(1)}, bf16[256,512]{0,1:T(8,128)(2,1)S(1)}, u32[]{:S(2)}, u32[]{:S(2)}) collective-permute-start(bf16[256,512]{0,1:T(8,128)(2,1)S(1)} %get-tuple-element.95), channel_id=1, source_target_pairs={{0,1},{1,0},{2,3},{3,2},{4,5},{5,4},{6,7},{7,6},{8,9},{9,8},{10,11... | collective-permute-start | bytes 786440 | tf_op jit(solution)/shard_map/ppermute | solution.py:661
  243.5 3.7 copy-start.21
  247.2 12.4 %copy-start.37 = (f32[256,1]{0,1:T(1,128)S(1)}, f32[256,1]{0,1:T(1,128)}, u32[]{:S(2)}) copy-start(f32[256,1]{0,1:T(1,128)} %constant_dynamic-slice_fusion.2) | copy-start | bytes 3076
  259.6 88.2 %copy-start.9 = (bf16[256,1024]{1,0:T(8,128)(2,1)}, bf16[256,1024]{1,0:T(8,128)(2,1)S(1)}, u32[]{:S(2)}) copy-start(bf16[256,1024]{1,0:T(8,128)(2,1)S(1)} %collective-permute-done.8) | copy-start | bytes 1572868
  350.5 10.4 %copy-start.26 = (f32[2,32,1408]{2,1,0:T(8,128)S(1)}, f32[2,32,1408]{2,1,0:T(8,128)}, u32[]{:S(2)}) copy-start(f32[2,32,1408]{2,1,0:T(8,128)} %get-tuple-element.34) | copy-start | bytes 1081348
  356.1 12.5 %copy-start.2 = (f32[256,1024]{1,0:T(8,128)S(1)}, f32[256,1024]{1,0:T(8,128)}, u32[]{:S(2)}) copy-start(f32[256,1024]{1,0:T(8,128)} %get-tuple-element.77) | copy-start | bytes 3145732
  364.3 6.8 %copy-start.31 = (f32[2,16,1024]{2,1,0:T(8,128)S(1)}, f32[2,16,1024]{2,1,0:T(8,128)}, u32[]{:S(2)}) copy-start(f32[2,16,1024]{2,1,0:T(8,128)} %get-tuple-element.32) | copy-start | bytes 393220
  (9 other events, 10.7 us)
